TPU v7x, 32 devices: a whole 2x2x4 slice. The times are simulated.
32 devices in a mesh: groups: 2 (over y), dp: 4 (over z), tgt: 4 (over x, core).
Axes of the slice: x: 2, y: 2, z: 4, core: 2. Of those that a mesh axis runs over, the one named last changes fastest.
Arguments:
- hidden: bfloat16 [6144, 4096], P(('groups', 'dp', 'tgt')), parts along dimension 0, may hold values from -6 to 6
- cotangent: bfloat16 [6144, 4096], P(('groups', 'dp', 'tgt')), parts along dimension 0, may hold values from -6 to 6
- adapter_down_weight: bfloat16 [4096, 64], replicated, may hold values from -0.09375 to 0.09375
- adapter_up_weight: bfloat16 [64, 4096], replicated, may hold values from -0.75 to 0.75
- width_projection_factor: bfloat16 [4096, 512], replicated, may hold values from -0.09375 to 0.09375
- rank_projection_factor: bfloat16 [64, 8], replicated, may hold values from -0.75 to 0.75
- targets: bfloat16 [8, 768, 8192], P(('groups', 'dp'), 'tgt'), parts along dimension 0, may hold values from -100 to 100
- strata: int32 [768], P(('groups', 'dp', 'tgt')), parts along dimension 0, may hold values from 0 to 31
- keep: int32 [768], P(('groups', 'dp', 'tgt')), parts along dimension 0, may hold values from 0 to 1
- shard_example_count: int32 [32], P(('groups', 'dp', 'tgt')), parts along dimension 0, may hold values from 18 to 24
- stratum_owner_table: int32 [32], replicated, may hold values from 0 to 3, as said below
Outputs:
- selection: float32 [768], P(('groups', 'dp', 'tgt')), parts along dimension 0
There are 2 independent parts, one for each index of `groups`. A program takes and returns all parts, laid end to end along the dimension named above; an argument that names none is the same for every part. Nothing has to cross between parts.
Inputs may be any that keep to these rules, and one draw needn't show every extreme that they name: `stratum_owner_table`: each of the 4 owners holds exactly 8 strata.
All inputs are finite; a program needn't handle non-finite values.
Results may differ from a plain program's by a relative error of at most 0.0029.
Values may be sent and summed in bfloat16 or wider, within the bound.
A program may use at most 64 MiB of HBM per device.

v0:
```python
import math

import jax
import jax.numpy as jnp
from jax import lax
from jax.sharding import PartitionSpec as P

FEAT = 8192
CAP = 2
TGT = 768
TASKS = 16


epsilon = 1e-06


def contracted_row_sums(row_block, col_block):
    return lax.dot_general(
        row_block, col_block, (((1,), (1,)), ((), ())), preferred_element_type=jnp.float32
    )


def inverse_norms(values):
    widened = values.astype(jnp.float32)
    return lax.rsqrt(jnp.sum(widened * widened, axis=1) + epsilon)


def task_terms(row_block, row_inv, col_block, col_inv, first_index):
    per_task = TGT // TASKS
    products = contracted_row_sums(row_block, col_block)
    aligned = math.sqrt(FEAT) * products * row_inv[:, None] * col_inv[None, :]
    target_ids = (first_index + jnp.arange(col_block.shape[0], dtype=jnp.int32)) // per_task
    task_mask = (target_ids[:, None] == jnp.arange(TASKS, dtype=jnp.int32)[None, :]).astype(
        jnp.float32
    )
    return jnp.dot(jnp.maximum(aligned, 0.0), task_mask, precision=lax.Precision.HIGHEST)


def per_example(values, examples):
    return values.reshape(examples, -1, values.shape[1])


def shards(
    hidden,
    cotangent,
    adapter_down_weight,
    adapter_up_weight,
    width_projection_factor,
    rank_projection_factor,
    targets,
    strata,
    keep,
    shard_example_count,
    stratum_owner_table,
):
    examples = strata.shape[0]
    strata_total = stratum_owner_table.shape[0]
    ordinal = jnp.arange(examples, dtype=jnp.int32)
    usable = ordinal < shard_example_count[0]
    is_live = jnp.logical_and(keep == 1, usable)
    member = strata[:, None] == jnp.arange(strata_total, dtype=jnp.int32)[None, :]
    local_counts = jnp.sum(jnp.logical_and(member, is_live[:, None]).astype(jnp.float32), axis=0)
    counts = lax.psum(local_counts, ("dp", "tgt"))
    down_activation = jnp.dot(
        hidden, adapter_down_weight, preferred_element_type=jnp.float32
    ).astype(jnp.bfloat16)
    up_backward_product = contracted_row_sums(cotangent, adapter_up_weight).astype(jnp.bfloat16)
    wide_hidden = jnp.dot(
        hidden, width_projection_factor, preferred_element_type=jnp.float32
    ).astype(jnp.bfloat16)
    wide_back = jnp.dot(
        cotangent, width_projection_factor, preferred_element_type=jnp.float32
    ).astype(jnp.bfloat16)
    rank_down = jnp.dot(
        down_activation, rank_projection_factor, preferred_element_type=jnp.float32
    ).astype(jnp.bfloat16)
    rank_up = jnp.dot(
        up_backward_product, rank_projection_factor, preferred_element_type=jnp.float32
    ).astype(jnp.bfloat16)
    up_grad = jnp.einsum(
        "esr,esd->erd",
        per_example(rank_down, examples),
        per_example(wide_back, examples),
        preferred_element_type=jnp.float32,
    )
    down_grad = jnp.einsum(
        "esd,esr->edr",
        per_example(wide_hidden, examples),
        per_example(rank_up, examples),
        preferred_element_type=jnp.float32,
    )
    features = jnp.concatenate(
        [up_grad.reshape(examples, -1), down_grad.reshape(examples, -1)], axis=1
    ).astype(jnp.bfloat16)
    owner_of = jnp.sum(jnp.where(member, stratum_owner_table[None, :], 0), axis=1)
    earlier = ordinal[:, None] > ordinal[None, :]
    same_owner = owner_of[:, None] == owner_of[None, :]
    ahead = jnp.logical_and(jnp.logical_and(earlier, same_owner), is_live[None, :])
    slot_rank = jnp.sum(ahead.astype(jnp.int32), axis=1)
    is_sent = jnp.logical_and(is_live, slot_rank < CAP)
    owner_count = lax.axis_size("dp")
    slot_index = owner_of * CAP + slot_rank
    slot_ids = jnp.arange(owner_count * CAP, dtype=jnp.int32)
    dispatch = jnp.logical_and(slot_ids[:, None] == slot_index[None, :], is_sent[None, :])
    outgoing = jnp.dot(
        dispatch.astype(jnp.bfloat16), features, preferred_element_type=jnp.float32
    ).astype(jnp.bfloat16)
    received = lax.all_to_all(
        outgoing.reshape(owner_count, CAP, -1), "dp", split_axis=0, concat_axis=0, tiled=True
    )
    owner_rows = received.reshape(owner_count * CAP, -1)
    own_targets = targets[0]
    target_inv = inverse_norms(own_targets)
    offset = lax.axis_index("tgt") * own_targets.shape[0]
    row_piece = lax.all_gather(owner_rows, "tgt", axis=0, tiled=True)
    partials = task_terms(row_piece, inverse_norms(row_piece), own_targets, target_inv, offset)
    task_sums = lax.psum_scatter(partials, "tgt", scatter_dimension=0, tiled=True)
    raw_owner = jnp.max(task_sums / (TGT // TASKS), axis=1)
    returned = lax.all_to_all(
        raw_owner.reshape(owner_count, CAP), "dp", split_axis=0, concat_axis=0, tiled=True
    ).reshape(owner_count * CAP)
    raw_score = jnp.sum(jnp.where(dispatch, returned[:, None], 0.0), axis=0)
    stratum_count = jnp.sum(jnp.where(member, counts[None, :], 0.0), axis=1)
    weight = jnp.sqrt(jnp.sum(counts) / (strata_total * jnp.maximum(stratum_count, 1.0)))
    return jnp.where(is_sent, raw_score * weight, 0.0)


def solution(mesh):
    return jax.shard_map(
        shards,
        mesh=mesh,
        in_specs=(
            P(("groups", "dp", "tgt"), None),
            P(("groups", "dp", "tgt"), None),
            P(),
            P(),
            P(),
            P(),
            P(("groups", "dp"), "tgt", None),
            P(("groups", "dp", "tgt")),
            P(("groups", "dp", "tgt")),
            P(("groups", "dp", "tgt")),
            P(),
        ),
        out_specs=P(("groups", "dp", "tgt")),
        check_vma=False,
    )
```

profile of v0, /device:TPU:0, one launch (start us, length us, event | category | flops | bytes accessed | tf_op | source)
XLA Modules:
  0.0 93.7 jit_solution(1229232755631329175)
XLA Ops:
  0.8 0.7 compare_and_fusion.1
  1.4 0.9 select_reduce_fusion.1
  2.5 0.7 compare_and_fusion
  3.2 2.3 %fusion.15 = bf16[192,8]{0,1:T(8,128)(2,1)S(1)} fusion(bf16[64,8]{0,1:T(8,128)(2,1)} %param.16, bf16[192,4096]{1,0:T(8,128)(2,1)} %param.12, bf16[64,4096]{1,0:T(8,128)(2,1)} %param.14), kind=kOutput, calls=%fused_computation.17 | convolution fusion | flops 100873728 | bytes 2101248 | tf_op jit(solution)/shard_map/dot_general | solution.py:77
  5.6 3.3 %convolution_convert_fusion.1 = bf16[24,512,8]{1,2,0:T(8,128)(2,1)S(1)} fusion(bf16[192,4096]{1,0:T(8,128)(2,1)S(1)} %copy-done, bf16[4096,512]{1,0:T(8,128)(2,1)} %param.15, bf16[24,8,8]{1,0,2:T(8,128)(2,1)S(1)} %reshape.70), kind=kOutput, calls=%fused_computation.4 | convolution fusion | flops 807075840 | bytes 5966848 | tf_op jit(solution)/shard_map/esd,esr->edr/dot_general | solution.py:86
  8.9 0.8 copy.25
  9.8 0.3 copy.26
  10.1 1.9 %fusion.16 = bf16[192,8]{0,1:T(8,128)(2,1)S(1)} fusion(bf16[64,8]{0,1:T(8,128)(2,1)S(1)} %copy-done.2, bf16[192,4096]{1,0:T(8,128)(2,1)S(1)} %copy-done, bf16[4096,64]{0,1:T(8,128)(2,1)} %param.13), kind=kOutput, calls=%fused_computation.18 | convolution fusion | flops 100873728 | bytes 2101248 | tf_op jit(solution)/shard_map/dot_general | solution.py:74
  12.0 0.7 reshape.66
  12.8 3.3 %convolution_convert_fusion.3 = bf16[24,8,512]{2,1,0:T(8,128)(2,1)S(1)} fusion(bf16[192,4096]{1,0:T(8,128)(2,1)S(1)} %copy-done.1, bf16[4096,512]{1,0:T(8,128)(2,1)} %param.15, bf16[24,8,8]{1,0,2:T(8,128)(2,1)} %reshape.66), kind=kOutput, calls=%fused_computation.6 | convolution fusion | flops 807075840 | bytes 5966848 | tf_op jit(solution)/shard_map/esr,esd->erd/dot_general | solution.py:80
  16.4 0.7 reshape.72
  17.1 6.3 %all-to-all-start = ((bf16[4,2,8192]{2,1,0:T(2,128)(2,1)}), bf16[4,2,8192]{2,1,0:T(2,128)(2,1)S(1)}, u32[]{:S(2)}, u32[]{:S(2)}) async-start(bf16[4,2,8192]{2,1,0:T(2,128)(2,1)} %reshape.72), calls=%async_computation | async-start | bytes 262144 | tf_op jit(solution)/shard_map/all_to_all | solution.py:108
  23.5 0.7 convert_reduce_fusion
  24.2 2.6 %multiply_reduce_fusion = f32[192]{0:T(256)S(1)} fusion(bf16[1,192,8192]{2,1,0:T(8,128)(2,1)} %param.17), kind=kLoop, calls=%fused_computation.1 | loop fusion | flops 4718400 | bytes 3146496 | tf_op jit(solution)/shard_map/reduce_sum | solution.py:25
  26.9 33.1 %psum.7 = f32[32]{0:T(128)S(1)} all-reduce(f32[32]{0:T(128)S(1)} %convert_reduce_fusion), channel_id=1, replica_groups=mesh['groups'=2,'dp'=4,'tgt'=4] {'dp','tgt'}, use_global_device_ids=true, to_apply=%region_8.9 | all-reduce | flops 32 | bytes 256 | tf_op jit(solution)/shard_map/psum | solution.py:63
  60.2 0.6 reduce_sum.78
  60.8 0.6 dynamic-slice
  62.1 6.5 %all_gather.3 = bf16[32,8192]{1,0:T(8,128)(2,1)S(1)} all-gather(bf16[8,8192]{1,0:T(8,128)(2,1)S(1)} %reshape.73), channel_id=1, replica_groups=mesh['groups'=2,'dp'=4,'tgt'=4] {'tgt'}, dimensions={0}, use_global_device_ids=true | all-gather | bytes 655360 | tf_op jit(solution)/shard_map/all_gather | solution.py:115
  68.8 3.0 %fusion.10 = f32[32,192]{1,0:T(8,128)S(1)} fusion(bf16[32,8192]{1,0:T(8,128)(2,1)S(1)} %all_gather.3, bf16[1,192,8192]{2,1,0:T(8,128)(2,1)} %param.17, f32[192]{0:T(256)S(1)} %add_rsqrt_fusion, f32[32]{0:T(128)S(1)} %rsqrt_multiply_fusion), kind=kOutput, calls=%fused_computation.14 | convolution fusion | flops 100681728 | bytes 3695488 | tf_op jit(solution)/shard_map/dot_general | solution.py:18
  72.0 11.1 %all-reduce = f32[32,16]{1,0:T(8,128)S(1)} all-reduce(f32[32,16]{1,0:T(8,128)S(1)} %fusion.20), channel_id=2, replica_groups=mesh['groups'=2,'dp'=4,'tgt'=4] {'tgt'}, use_global_device_ids=true, to_apply=%region_4.5.clone | all-reduce | flops 512 | bytes 4096
  83.4 7.9 %all_to_all.14 = f32[4,1,2]{2,1,0:T(1,128)S(1)} all-to-all(f32[4,1,2]{2,1,0:T(1,128)S(1)} %bitcast.45), channel_id=1, replica_groups=mesh['groups'=2,'dp'=4,'tgt'=4] {'dp'}, dimensions={0} | all-to-all | bytes 64 | tf_op jit(solution)/shard_map/all_to_all | solution.py:119
  91.3 0.5 broadcast.76
  91.8 0.7 reduce.3
  92.6 1.1 %multiply_select_fusion = f32[24]{0:T(128)} fusion(pred[24]{0:T(512)(128)(4,1)S(1)} %compare_and_fusion, f32[24]{0:T(128)S(1)} %select_reduce_fusion.2, f32[24]{0:T(128)S(1)} %select_reduce_fusion, f32[]{:T(128)} %reduce_sum.78), kind=kLoop, calls=%fused_computation.48 | loop fusion | flops 120 | bytes 316 | tf_op jit(solution)/shard_map/jit(_where)/select_n | solution.py:125
  (27 shorter events, 1.7 us)
Async XLA Ops:
  0.0 5.6 %copy-start = (bf16[192,4096]{1,0:T(8,128)(2,1)S(1)}, bf16[192,4096]{1,0:T(8,128)(2,1)}, u32[]{:S(2)}) copy-start(bf16[192,4096]{1,0:T(8,128)(2,1)} %param.11) | copy-start | bytes 4718596
  8.9 1.2 %copy-start.2 = (bf16[64,8]{0,1:T(8,128)(2,1)S(1)}, bf16[64,8]{0,1:T(8,128)(2,1)}, u32[]{:S(2)}) copy-start(bf16[64,8]{0,1:T(8,128)(2,1)} %param.16) | copy-start | bytes 3076
  10.1 2.7 %copy-start.1 = (bf16[192,4096]{1,0:T(8,128)(2,1)S(1)}, bf16[192,4096]{1,0:T(8,128)(2,1)}, u32[]{:S(2)}) copy-start(bf16[192,4096]{1,0:T(8,128)(2,1)} %param.12) | copy-start | bytes 4718596
  17.1 44.9 %all-to-all-start = ((bf16[4,2,8192]{2,1,0:T(2,128)(2,1)}), bf16[4,2,8192]{2,1,0:T(2,128)(2,1)S(1)}, u32[]{:S(2)}, u32[]{:S(2)}) async-start(bf16[4,2,8192]{2,1,0:T(2,128)(2,1)} %reshape.72), calls=%async_computation | async-start | bytes 262144 | tf_op jit(solution)/shard_map/all_to_all | solution.py:108
  24.2 35.8 %copy-start.3 = (s32[24]{0:T(128)S(1)}, s32[24]{0:T(128)}, u32[]{:S(2)}) copy-start(s32[24]{0:T(128)} %param.18) | copy-start | bytes 292
  24.2 36.5 %copy-start.4 = (u32[32]{0:T(128)S(1)}, u32[32]{0:T(128)}, u32[]{:S(2)}) copy-start(u32[32]{0:T(128)} %constant.44) | copy-start | bytes 388
where the time goes:
time: 94.3 us; the launch traced here: 93.7 us
  blocking collectives  58.7 us (62%)
  matrix products  14.3 us (15%)
  other arithmetic  8.73 us (9%)
  starting transfers between devices  6.34 us (7%)
  local copies, waits for them, and re-layouts  4.17 us (4%)
  between operations  1.57 us (2%)
    psum x1, blocking collectives, shards(): counts = lax.psum(local_counts, ('dp', 'tgt'))  33.1 us
    unnamed x1, blocking collectives  11.1 us
    all_to_all x1, blocking collectives, shards(): lax.all_to_all(raw_owner.reshape(owner_count, CAP), 'dp', split_axis=0, c...  7.9 us
    all_gather x1, blocking collectives, shards(): row_piece = lax.all_gather(owner_rows, 'tgt', axis=0, tiled=True)  6.5 us
    all_to_all x1, starting transfers between devices, shards(): lax.all_to_all(outgoing.reshape(owner_count, CAP, -1), 'dp', split_axis=0...  6.34 us
    dot_general x1, matrix products, shards(): jnp.einsum('esr,esd->erd', per_example(rank_down, examples), per_example(...  3.33 us
    dot_general x1, matrix products, shards(): jnp.einsum('esd,esr->edr', per_example(wide_hidden, examples), per_exampl...  3.31 us
    dot_general x1, matrix products, contracted_row_sums(): lax.dot_general(row_block, col_block, (((1,), (1,)), ((), ())), preferred...  2.97 us
  transfers between devices with their start and end apart: 1, of which 0 were waited for; matrix products, arithmetic and copies ran while one was open for 5% of the time, Pallas kernels for 0%

commit v1 on v0

v1 whole, which is shorter than its diff:
```python
import math

import jax
import jax.numpy as jnp
from jax import lax
from jax.experimental import pallas as pl
from jax.experimental.pallas import tpu as pltpu
from jax.sharding import PartitionSpec as P

CAP = 2
TASKS = 16
EPSILON = 1e-06
CORES = 2
CHUNKS = 4
HALVES = 2

F32 = jnp.float32
BF16 = jnp.bfloat16
I32 = jnp.int32
MESH = pl.DeviceIdType.MESH


def dot(a, b):
    return jnp.dot(a, b, preferred_element_type=F32)


def dot_nt(a, b):
    return lax.dot_general(a, b, (((1,), (1,)), ((), ())), preferred_element_type=F32)


def iota(shape, axis):
    return lax.broadcasted_iota(I32, shape, axis)


def column_of(row):
    size = row.shape[1]
    eye = iota((size, size), 0) == iota((size, size), 1)
    return jnp.sum(jnp.where(eye, jnp.broadcast_to(row, (size, size)), 0.0), axis=1, keepdims=True)


def each(start, stop, body):
    if stop - start <= 32:
        for k in range(start, stop):
            body(k)
    else:
        lax.fori_loop(start, stop, lambda k, c: (body(k), c)[1], 0)


def partner(z, k, nz):
    if nz & (nz - 1):
        return lax.rem(z + k, nz)
    bit = 1
    while bit < nz:
        if k & bit:
            z = z + bit - 2 * bit * lax.rem(z // bit, 2)
        bit *= 2
    return z


def kernel(nz, nt, hid_h, cot_h, ad_h, au_h, w_h, rp_ref, tg_h, strata_ref, keep_ref,
           cnt_ref, table_ref, out_ref, hid, cot, ad, au, wf, tup, tdr, tdn, sel, sbuf, xbuf,
           acc, crow, cbuf, rrow, rbuf, in_sem, tg_sem, zs, zr, xs, xr, cs, cr, ns, nr, rs, rr):
    n = nz * nt
    nx = nt // CORES
    z = lax.axis_index("dp")
    t = lax.axis_index("tgt")
    me = z * nt + t
    x, c = t // CORES, lax.rem(t, CORES)
    tokens, width = hid.shape
    kd = wf.shape[1]
    hw = kd // HALVES
    kr = rp_ref.shape[1]
    examples = strata_ref.shape[1]
    seq = tokens // examples
    strata_total = table_ref.shape[1]
    local_targets = tdr.shape[0]
    slots = nz * CAP
    rows = slots * kr
    kc = width // CHUNKS

    def peer(j):
        return {"dp": j // nt, "tgt": lax.rem(j, nt)}

    def loads(k):
        ks = pl.ds(k * kc, kc)
        return [
            pltpu.make_async_copy(hid_h.at[:, ks], hid.at[:, ks], in_sem.at[0, k]),
            pltpu.make_async_copy(w_h.at[ks, pl.ds(0, hw)], wf.at[ks, pl.ds(0, hw)], in_sem.at[1, k]),
            pltpu.make_async_copy(cot_h.at[:, ks], cot.at[:, ks], in_sem.at[2, k]),
            pltpu.make_async_copy(ad_h.at[ks, :], ad.at[ks, :], in_sem.at[3, k]),
            pltpu.make_async_copy(au_h.at[:, ks], au.at[:, ks], in_sem.at[4, k]),
        ]

    def late_loads(k):
        ks = pl.ds(k * kc, kc)
        rest = pl.ds(hw, kd - hw)
        return [pltpu.make_async_copy(w_h.at[ks, rest], wf.at[ks, rest], in_sem.at[5, k])]

    first = [loads(k) for k in range(CHUNKS)]
    second = [late_loads(k) for k in range(CHUNKS)]
    up_len = kr * kd
    target_loads = [
        pltpu.make_async_copy(tg_h.at[0, :, pl.ds(r * kd, kd)], tup.at[r], tg_sem.at[r])
        for r in range(kr)
    ] + [pltpu.make_async_copy(tg_h.at[0, :, pl.ds(up_len, up_len)], tdr, tg_sem.at[kr])]
    for group in first + second:
        for copy in group:
            copy.start()
    for copy in target_loads:
        copy.start()

    barrier = pltpu.get_barrier_semaphore()

    def greet(k):
        pl.semaphore_signal(barrier, inc=1, device_id=peer(lax.rem(me + k, n)), device_id_type=MESH)

    each(1, n, greet)

    strata = strata_ref[...].astype(F32)
    live = jnp.logical_and(keep_ref[...] == 1, iota((1, examples), 1) < cnt_ref[...])
    live_f = live.astype(F32)
    strata_c = column_of(strata)
    live_c = column_of(live_f)
    table_c = column_of(table_ref[...].astype(F32))
    member = strata == iota((strata_total, examples), 0).astype(F32)
    owner = jnp.sum(jnp.where(member, table_c, 0.0), axis=0, keepdims=True)
    owner_c = column_of(owner)
    earlier = iota((examples, examples), 0) < iota((examples, examples), 1)
    ahead = jnp.where(jnp.logical_and(earlier, owner_c == owner), live_c, 0.0)
    slot_rank = jnp.sum(ahead, axis=0, keepdims=True)
    sent = jnp.logical_and(live, slot_rank < float(CAP))
    slot = jnp.where(sent, owner * float(CAP) + slot_rank, -1.0)
    lanes = crow.shape[1]
    member_t = strata_c == iota((examples, lanes), 1).astype(F32)
    crow[...] = jnp.sum(jnp.where(member_t, live_c, 0.0), axis=0, keepdims=True)
    own_counts = crow[...]

    spread = (iota((examples, tokens), 1) // seq == iota((examples, tokens), 0)).astype(BF16)
    slot_tok = dot(jnp.broadcast_to(slot, (8, examples)).astype(BF16), spread)[0:1, :]
    row_slot = (iota((rows, tokens), 0) // kr).astype(F32)
    picked = row_slot == slot_tok
    row_rank = (
        lax.rem(iota((rows, kr), 0), kr) == iota((rows, kr), 1)
    ).astype(BF16)

    pl.semaphore_wait(barrier, n - 1)

    def count_copy(k):
        return pltpu.make_async_remote_copy(
            crow, cbuf.at[me], ns, nr, device_id=peer(lax.rem(me + k, n)), device_id_type=MESH)

    each(1, n, lambda k: count_copy(k).start())
    cbuf[me] = own_counts

    span = sel.shape[0]
    dd = span // kr
    src = iota((span, span), 0)
    dst = iota((span, span), 1)
    sel[...] = (src == lax.rem(dst, dd) * kr + dst // dd).astype(F32).astype(BF16)

    wide_h = wide_b = down = up = None
    for k in range(CHUNKS):
        for copy in first[k]:
            copy.wait()
        ks = pl.ds(k * kc, kc)
        h, b, w = hid[:, ks], cot[:, ks], wf[ks, 0:hw]
        terms = (dot(h, w), dot(b, w), dot(h, ad[ks, :]), dot_nt(b, au[:, ks]))
        if k == 0:
            wide_h, wide_b, down, up = terms
        else:
            wide_h, wide_b, down, up = [
                a + p for a, p in zip((wide_h, wide_b, down, up), terms)]
    rank_down = dot(down.astype(BF16), rp_ref[...]).astype(BF16)
    rank_up = dot(up.astype(BF16), rp_ref[...]).astype(BF16)
    mix_up = jnp.where(picked, dot_nt(row_rank, rank_down), 0.0).astype(BF16)
    mix_down = jnp.where(picked, dot_nt(row_rank, rank_up), 0.0).astype(BF16)

    def z_copy(half, k):
        to = partner(z, k, nz)
        return pltpu.make_async_remote_copy(
            sbuf.at[half, to], xbuf.at[half, c, x, z], zs.at[half], zr.at[half, z],
            device_id={"dp": to}, device_id_type=MESH)

    def x_copy(half, src_ref, origin_z, to_x):
        return pltpu.make_async_remote_copy(
            src_ref, xbuf.at[half, c, x, origin_z], xs.at[half], xr.at[half, x, origin_z],
            device_id={"tgt": to_x * CORES + c}, device_id_type=MESH)

    def c_copy(half, src_ref, origin_x, origin_z):
        return pltpu.make_async_remote_copy(
            src_ref, xbuf.at[half, c, origin_x, origin_z], cs.at[half], cr.at[half],
            device_id={"tgt": x * CORES + 1 - c}, device_id_type=MESH)

    def spread_out(half, src_ref, origin_z):
        for dx in range(1, nx):
            x_copy(half, src_ref, origin_z, lax.rem(x + dx, nx)).start()
        c_copy(half, src_ref, x, origin_z).start()

    def features(half, wb, wh):
        up_f = dot(mix_up, wb.astype(BF16)).astype(BF16)
        down_f = dot(mix_down, wh.astype(BF16)).astype(BF16)
        sbuf[half, :, :, 0:hw] = up_f.reshape(nz, CAP * kr, hw)
        sbuf[half, :, :, hw:2 * hw] = down_f.reshape(nz, CAP * kr, hw)
        for k in range(nz - 1, 0, -1):
            z_copy(half, k).start()
        spread_out(half, sbuf.at[half, z], z)
        xbuf[half, c, x, z] = sbuf[half, z]
        wide_u, wide_d = up_f.astype(F32), down_f.astype(F32)
        return jnp.sum(wide_u * wide_u + wide_d * wide_d, axis=1, keepdims=True)

    square = features(0, wide_b, wide_h)
    for k in range(CHUNKS):
        for copy in second[k]:
            copy.wait()
        ks = pl.ds(k * kc, kc)
        w = wf[ks, hw:kd]
        terms = (dot(hid[:, ks], w), dot(cot[:, ks], w))
        if k == 0:
            wide_h, wide_b = terms
        else:
            wide_h, wide_b = wide_h + terms[0], wide_b + terms[1]
    square = square + features(1, wide_b, wide_h)

    for copy in target_loads:
        copy.wait()
    total = None
    for r in range(kr):
        v = tup[r].astype(F32)
        total = v * v if total is None else total + v * v
    for q in range(up_len // kd):
        v = tdr[:, q * kd:(q + 1) * kd].astype(F32)
        total = total + v * v
    target_scale = math.sqrt(2.0 * up_len) * lax.rsqrt(
        jnp.sum(total, axis=1, keepdims=True) + EPSILON)

    def arrange(q):
        piece = dot(tdr[:, q * span:(q + 1) * span], sel[...]).astype(BF16)
        for r in range(kr):
            tdn[r, :, q * dd:(q + 1) * dd] = piece[:, r * dd:(r + 1) * dd]

    def relay_z(half, k):
        origin = partner(z, k, nz)
        pltpu.make_async_remote_copy(
            sbuf.at[half, origin], xbuf.at[half, c, x, origin], zs.at[half], zr.at[half, origin],
            device_id={"dp": origin}, device_id_type=MESH).wait_recv()
        spread_out(half, xbuf.at[half, c, x, origin], origin)

    def relay_x(half, dx, k):
        origin_x = lax.rem(x + dx, nx)
        origin_z = partner(z, k, nz)
        block = xbuf.at[half, c, origin_x, origin_z]
        pltpu.make_async_remote_copy(
            block, block, xs.at[half], xr.at[half, origin_x, origin_z],
            device_id={"tgt": origin_x * CORES + c}, device_id_type=MESH).wait_recv()
        c_copy(half, block, origin_x, origin_z).start()

    pieces = up_len // span
    todo = [lambda q=q: arrange(q) for q in range(pieces)]
    steps = []
    for half in range(HALVES):
        steps += [lambda half=half, k=k: relay_z(half, k) for k in range(1, nz)]
    done = 0
    for i, step in enumerate(steps):
        while done < pieces and done * len(steps) <= i * pieces:
            todo[done]()
            done += 1
        step()
    while done < pieces:
        todo[done]()
        done += 1
    for half in range(HALVES):
        for dx in range(1, nx):
            for k in range(nz):
                relay_x(half, dx, k)

    count = nx * nz * CORES * CAP * kr
    lane = iota((local_targets, count), 1)
    lane_rank = lax.rem(lane, kr)
    for half in range(HALVES):
        other = xbuf.at[half, 1 - c]
        pltpu.make_async_copy(other, other, cr.at[half]).wait()
        block = xbuf[half].reshape(count, 2 * hw)
        cols = slice(half * hw, (half + 1) * hw)
        left = tup[:, :, cols].reshape(kr * local_targets, hw)
        right = tdn[:, :, cols].reshape(kr * local_targets, hw)
        products = dot_nt(left, block[:, 0:hw]) + dot_nt(right, block[:, hw:2 * hw])
        products = products.reshape(kr, local_targets, count)
        s = products[0]
        for r in range(1, kr):
            s = jnp.where(lane_rank == r, products[r], s)
        if half == 0:
            acc[...] = s
        else:
            s = acc[...] + s
    shift = 1
    while shift < kr:
        s = s + pltpu.roll(s, count - shift, 1)
        shift *= 2
    per_task = local_targets * nt // TASKS
    s = jnp.maximum(s * target_scale, 0.0)
    local_tasks = local_targets // per_task
    best = jnp.sum(s[0:per_task], axis=0, keepdims=True)
    for k in range(1, local_tasks):
        best = jnp.maximum(
            best, jnp.sum(s[k * per_task:(k + 1) * per_task], axis=0, keepdims=True))
    rrow[...] = best / float(per_task)

    def score_copy(k):
        return pltpu.make_async_remote_copy(
            rrow, rbuf.at[me], rs, rr, device_id=peer(lax.rem(me + k, n)), device_id_type=MESH)

    each(1, n, lambda k: score_copy(k).start())
    rbuf[me] = rrow[...]

    counts_all = cbuf.at[pl.ds(0, n - 1)]
    pltpu.make_async_copy(counts_all, counts_all, nr).wait()
    counts = jnp.sum(cbuf[...], axis=0)
    overall = jnp.sum(counts, axis=1, keepdims=True)
    stratum_c = jnp.sum(jnp.where(member_t, counts, 0.0), axis=1, keepdims=True)
    weight_c = jnp.sqrt(overall / (float(strata_total) * jnp.maximum(stratum_c, 1.0)))
    eye = iota((examples, examples), 0) == iota((examples, examples), 1)
    weight = jnp.sum(jnp.where(eye, weight_c, 0.0), axis=0, keepdims=True)
    at_slot = (iota((rows, examples), 0) // kr).astype(F32) == slot
    square_e = jnp.sum(jnp.where(at_slot, square, 0.0), axis=0, keepdims=True)
    weight = weight * lax.rsqrt(square_e + EPSILON)

    scores_all = rbuf.at[pl.ds(0, n - 1)]
    pltpu.make_async_copy(scores_all, scores_all, rr).wait()
    home = ((c * nx + x) * nz + z) * CAP * kr
    raw = jnp.zeros((1, examples), F32)
    lane_row = iota((1, count), 1)
    for o in range(nz):
        top = jnp.max(rbuf[o * nt:(o + 1) * nt], axis=0)
        for rank in range(CAP):
            mine = jnp.sum(
                jnp.where(lane_row == home + rank * kr, top, 0.0), axis=1, keepdims=True)
            raw = jnp.where(slot == float(o * CAP + rank), mine, raw)
    out_ref[...] = jnp.where(sent, raw * weight, 0.0)

    def drain(ref, sem):
        pltpu.make_async_copy(ref, ref, sem).wait()

    drain(counts_all, ns)
    drain(scores_all, rs)
    for half in range(HALVES):
        if nz > 1:
            drain(sbuf.at[half, pl.ds(0, nz - 1)], zs.at[half])
        for _ in range(1, nx):
            drain(xbuf.at[half, 0, 0], xs.at[half])
        drain(xbuf.at[half, 0], cs.at[half])


def solution(mesh):
    nz, nt = mesh.shape["dp"], mesh.shape["tgt"]

    def shards(hidden, cotangent, adapter_down_weight, adapter_up_weight, width_projection_factor,
               rank_projection_factor, targets, strata, keep, shard_example_count,
               stratum_owner_table):
        tokens, width = hidden.shape
        rank, kr = rank_projection_factor.shape
        kd = width_projection_factor.shape[1]
        examples = strata.shape[0]
        strata_total = stratum_owner_table.shape[0]
        local_targets, feat = targets.shape[1:]
        n, nx = nz * nt, nt // CORES
        count = n * CAP * kr
        span = kr * 128
        count_lanes = -(-strata_total // 128) * 128
        dma = pltpu.SemaphoreType.DMA
        hbm = pl.BlockSpec(memory_space=pl.ANY)
        vmem = pl.BlockSpec(memory_space=pltpu.VMEM)

        def body(*refs):
            kernel(nz, nt, *refs)

        out = pl.pallas_call(
            body,
            name="select",
            out_shape=jax.ShapeDtypeStruct((1, examples), F32),
            in_specs=[hbm, hbm, hbm, hbm, hbm, vmem, hbm, vmem, vmem, vmem, vmem],
            out_specs=vmem,
            scratch_shapes=[
                pltpu.VMEM((tokens, width), BF16),
                pltpu.VMEM((tokens, width), BF16),
                pltpu.VMEM((width, rank), BF16),
                pltpu.VMEM((rank, width), BF16),
                pltpu.VMEM((width, kd), BF16),
                pltpu.VMEM((kr, local_targets, kd), BF16),
                pltpu.VMEM((local_targets, feat // 2), BF16),
                pltpu.VMEM((kr, local_targets, kd), BF16),
                pltpu.VMEM((span, span), BF16),
                pltpu.VMEM((HALVES, nz, CAP * kr, 2 * kd // HALVES), BF16),
                pltpu.VMEM((HALVES, CORES, nx, nz, CAP * kr, 2 * kd // HALVES), BF16),
                pltpu.VMEM((local_targets, count), F32),
                pltpu.VMEM((1, count_lanes), F32),
                pltpu.VMEM((n, 1, count_lanes), F32),
                pltpu.VMEM((1, count), F32),
                pltpu.VMEM((n, 1, count), F32),
                dma((6, CHUNKS)),
                dma((kr + 1,)),
                dma((HALVES,)),
                dma((HALVES, nz)),
                dma((HALVES,)),
                dma((HALVES, nx, nz)),
                dma((HALVES,)),
                dma((HALVES,)),
                dma,
                dma,
                dma,
                dma,
            ],
            compiler_params=pltpu.CompilerParams(
                collective_id=0, has_side_effects=True, vmem_limit_bytes=60 * 1024 * 1024),
        )(hidden, cotangent, adapter_down_weight, adapter_up_weight, width_projection_factor,
          rank_projection_factor, targets, strata.reshape(1, -1), keep.reshape(1, -1),
          shard_example_count.reshape(1, 1), stratum_owner_table.reshape(1, -1))
        return out.reshape(-1)

    split = P(("groups", "dp", "tgt"))
    rows = P(("groups", "dp", "tgt"), None)
    return jax.shard_map(
        shards,
        mesh=mesh,
        in_specs=(rows, rows, P(), P(), P(), P(), P(("groups", "dp"), "tgt", None),
                  split, split, split, P()),
        out_specs=split,
        check_vma=False,
    )
```

time: 94.3 us -> 31.4 us (0.33)
  blocking collectives: 58.7 us -> 0 us
  Pallas kernels: 0 us -> 25.6 us
  matrix products: 14.3 us -> 0 us
  other arithmetic: 8.73 us -> 0 us
  starting transfers between devices: 6.34 us -> 0 us
    psum x1 -> x0, blocking collectives: 33.1 us -> none  [shards(): counts = lax.psum(local_counts, ('dp', 'tgt'))]
    pallas_call x0 -> x1, Pallas kernels: none -> 25.6 us  [shards(): pl.pallas_call(body, name='select', out_shape=jax.ShapeDtypeStruct((1, ex...]
    dot_general x7 -> x0, matrix products: 14.3 us -> none  [the longest x1 3.33 us: shards(): jnp.einsum('esr,esd->erd', per_example(rank_down, examples), per_example(...]
    unnamed x1 -> x0, blocking collectives: 11.1 us -> none
    all_to_all x1 -> x0, blocking collectives: 7.9 us -> none  [shards(): lax.all_to_all(raw_owner.reshape(owner_count, CAP), 'dp', split_axis=0, c...]
    all_gather x1 -> x0, blocking collectives: 6.5 us -> none  [shards(): row_piece = lax.all_gather(owner_rows, 'tgt', axis=0, tiled=True)]
    all_to_all x1 -> x0, starting transfers between devices: 6.34 us -> none  [shards(): lax.all_to_all(outgoing.reshape(owner_count, CAP, -1), 'dp', split_axis=0...]
    reduce_sum x8 -> x0, other arithmetic: 5.49 us -> none  [the longest x2 2.85 us: inverse_norms(): return lax.rsqrt(jnp.sum(widened * widened, axis=1) + epsilon)]
  transfers between devices with their start and end apart: 1 -> 0, of which waited for: 0 -> 0; matrix products, arithmetic and copies ran while one was open for 5% -> 0% of each run, Pallas kernels for 0% -> 0%
where the time goes in v1:
time: 31.4 us; the launch traced here: 31.1 us
  Pallas kernels  25.6 us (82%)
  local copies, waits for them, and re-layouts  4.86 us (15%)
  between operations  0.66 us (2%)
    pallas_call x1, Pallas kernels, shards(): pl.pallas_call(body, name='select', out_shape=jax.ShapeDtypeStruct((1, ex...  25.6 us
    unnamed x3, local copies, waits for them, and re-layouts  4.86 us

profile of v1, /device:TPU:0, one launch (start us, length us, event | category | flops | bytes accessed | tf_op | source)
XLA Modules:
  0.0 31.1 jit_solution(14671267864500455450)
XLA Ops:
  0.7 1.4 %copy.13.refs_5_ = bf16[64,8]{1,0:T(8,128)(2,1)} copy(bf16[64,8]{0,1:T(8,128)(2,1)} %param.16) | data formatting | bytes 2048 | tf_op args[5]
  2.0 2.4 %copy.12.refs_2_ = bf16[4096,64]{1,0:T(8,128)(2,1)} copy(bf16[4096,64]{0,1:T(8,128)(2,1)} %param.13) | data formatting | bytes 1048576 | tf_op args[2]
  4.4 25.6 %select.1 = f32[1,24]{1,0:T(1,128)} custom-call(bf16[192,4096]{1,0:T(8,128)(2,1)} %refs_0_.1, bf16[192,4096]{1,0:T(8,128)(2,1)} %refs_1_.1, bf16[4096,64]{1,0:T(8,128)(2,1)} %copy.12.refs_2_, bf16[64,4096]{1,0:T(8,128)(2,1)} %refs_3_.1, bf16[4096,512]{1,0:T(8,128)(2,1)} %refs_4_.1, bf16[64,8]{1,0:T(8,128)(2,1)} %copy.13.refs_5_, ...), custom_call_target="tpu_custom_call" | custom-call | tf_op jit(solution)/shard_map/select/pallas_call | solution.py:376
  30.0 1.1 %copy.16 = f32[24]{0:T(128)} copy(f32[24]{0:T(128)} %bitcast.9) | data formatting | bytes 192

commit v2 on v1

--- a/solution.py
+++ b/solution.py
@@ -69,7 +69,7 @@
     tokens, width = hid.shape
     kd = wf.shape[1]
     hw = kd // HALVES
-    kr = rp_ref.shape[1]
+    kr = rp_ref.shape[0]
     examples = strata_ref.shape[1]
     seq = tokens // examples
     strata_total = table_ref.shape[1]
@@ -87,7 +87,7 @@
             pltpu.make_async_copy(hid_h.at[:, ks], hid.at[:, ks], in_sem.at[0, k]),
             pltpu.make_async_copy(w_h.at[ks, pl.ds(0, hw)], wf.at[ks, pl.ds(0, hw)], in_sem.at[1, k]),
             pltpu.make_async_copy(cot_h.at[:, ks], cot.at[:, ks], in_sem.at[2, k]),
-            pltpu.make_async_copy(ad_h.at[ks, :], ad.at[ks, :], in_sem.at[3, k]),
+            pltpu.make_async_copy(ad_h.at[:, ks], ad.at[:, ks], in_sem.at[3, k]),
             pltpu.make_async_copy(au_h.at[:, ks], au.at[:, ks], in_sem.at[4, k]),
         ]
 
@@ -117,7 +117,7 @@
     each(1, n, greet)
 
     strata = strata_ref[...].astype(F32)
-    live = jnp.logical_and(keep_ref[...] == 1, iota((1, examples), 1) < cnt_ref[...])
+    live = jnp.logical_and(keep_ref[...] == 1, iota((1, examples), 1) < cnt_ref[0])
     live_f = live.astype(F32)
     strata_c = column_of(strata)
     live_c = column_of(live_f)
@@ -154,9 +154,9 @@
 
     span = sel.shape[0]
     dd = span // kr
-    src = iota((span, span), 0)
-    dst = iota((span, span), 1)
-    sel[...] = (src == lax.rem(dst, dd) * kr + dst // dd).astype(F32).astype(BF16)
+    dst = iota((1, span), 1)
+    source = lax.rem(dst, dd) * kr + dst // dd
+    sel[...] = (iota((span, span), 0) == source).astype(F32).astype(BF16)
 
     wide_h = wide_b = down = up = None
     for k in range(CHUNKS):
@@ -164,14 +164,14 @@
             copy.wait()
         ks = pl.ds(k * kc, kc)
         h, b, w = hid[:, ks], cot[:, ks], wf[ks, 0:hw]
-        terms = (dot(h, w), dot(b, w), dot(h, ad[ks, :]), dot_nt(b, au[:, ks]))
+        terms = (dot(h, w), dot(b, w), dot_nt(h, ad[:, ks]), dot_nt(b, au[:, ks]))
         if k == 0:
             wide_h, wide_b, down, up = terms
         else:
             wide_h, wide_b, down, up = [
                 a + p for a, p in zip((wide_h, wide_b, down, up), terms)]
-    rank_down = dot(down.astype(BF16), rp_ref[...]).astype(BF16)
-    rank_up = dot(up.astype(BF16), rp_ref[...]).astype(BF16)
+    rank_down = dot_nt(down.astype(BF16), rp_ref[...]).astype(BF16)
+    rank_up = dot_nt(up.astype(BF16), rp_ref[...]).astype(BF16)
     mix_up = jnp.where(picked, dot_nt(row_rank, rank_down), 0.0).astype(BF16)
     mix_down = jnp.where(picked, dot_nt(row_rank, rank_up), 0.0).astype(BF16)
 
@@ -369,6 +369,7 @@
         dma = pltpu.SemaphoreType.DMA
         hbm = pl.BlockSpec(memory_space=pl.ANY)
         vmem = pl.BlockSpec(memory_space=pltpu.VMEM)
+        smem = pl.BlockSpec(memory_space=pltpu.SMEM)
 
         def body(*refs):
             kernel(nz, nt, *refs)
@@ -377,12 +378,12 @@
             body,
             name="select",
             out_shape=jax.ShapeDtypeStruct((1, examples), F32),
-            in_specs=[hbm, hbm, hbm, hbm, hbm, vmem, hbm, vmem, vmem, vmem, vmem],
+            in_specs=[hbm, hbm, hbm, hbm, hbm, vmem, hbm, vmem, vmem, smem, vmem],
             out_specs=vmem,
             scratch_shapes=[
                 pltpu.VMEM((tokens, width), BF16),
                 pltpu.VMEM((tokens, width), BF16),
-                pltpu.VMEM((width, rank), BF16),
+                pltpu.VMEM((rank, width), BF16),
                 pltpu.VMEM((rank, width), BF16),
                 pltpu.VMEM((width, kd), BF16),
                 pltpu.VMEM((kr, local_targets, kd), BF16),
@@ -411,9 +412,9 @@
             ],
             compiler_params=pltpu.CompilerParams(
                 collective_id=0, has_side_effects=True, vmem_limit_bytes=60 * 1024 * 1024),
-        )(hidden, cotangent, adapter_down_weight, adapter_up_weight, width_projection_factor,
-          rank_projection_factor, targets, strata.reshape(1, -1), keep.reshape(1, -1),
-          shard_example_count.reshape(1, 1), stratum_owner_table.reshape(1, -1))
+        )(hidden, cotangent, adapter_down_weight.T, adapter_up_weight, width_projection_factor,
+          rank_projection_factor.T, targets, strata.reshape(1, -1), keep.reshape(1, -1),
+          shard_example_count, stratum_owner_table.reshape(1, -1))
         return out.reshape(-1)
 
     split = P(("groups", "dp", "tgt"))

time: 31.4 us -> 27.4 us (0.87)
  local copies, waits for them, and re-layouts: 4.86 us -> 1.19 us
    unnamed x3 -> x1, local copies, waits for them, and re-layouts: 4.86 us -> 1.19 us
where the time goes in v2:
time: 27.4 us; the launch traced here: 27.3 us
  Pallas kernels  25.4 us (93%)
  local copies, waits for them, and re-layouts  1.19 us (4%)
  between operations  0.66 us (2%)
    pallas_call x1, Pallas kernels, shards(): pl.pallas_call(body, name='select', out_shape=jax.ShapeDtypeStruct((1, ex...  25.4 us
    unnamed x1, local copies, waits for them, and re-layouts  1.19 us

profile of v2, /device:TPU:0, one launch (start us, length us, event | category | flops | bytes accessed | tf_op | source)
XLA Modules:
  0.0 27.3 jit_solution(12937513828184704631)
XLA Ops:
  0.7 25.4 %select.1 = f32[1,24]{1,0:T(1,128)} custom-call(bf16[192,4096]{1,0:T(8,128)(2,1)} %refs_0_.1, bf16[192,4096]{1,0:T(8,128)(2,1)} %refs_1_.1, bf16[64,4096]{1,0:T(8,128)(2,1)} %bitcast.6, bf16[64,4096]{1,0:T(8,128)(2,1)} %refs_3_.1, bf16[4096,512]{1,0:T(8,128)(2,1)} %refs_4_.1, bf16[8,64]{1,0:T(8,128)(2,1)} %bitcast.7, bf16[1,192,8192]{2,1,0:T(8,128)(2,1)} %refs_6_.1, ...), custom_call_target="tpu_custom_call" | custom-call | tf_op jit(solution)/shard_map/select/pallas_call | solution.py:377
  26.1 1.2 %copy.14 = f32[24]{0:T(128)} copy(f32[24]{0:T(128)} %bitcast.11) | data formatting | bytes 192

commit v3 on v2

--- a/solution.py
+++ b/solution.py
@@ -81,6 +81,17 @@
     def peer(j):
         return {"dp": j // nt, "tgt": lax.rem(j, nt)}
 
+    barrier = pltpu.get_barrier_semaphore()
+    for k in range(nz - 1, 0, -1):
+        pl.semaphore_signal(
+            barrier, inc=1, device_id={"dp": partner(z, k, nz)}, device_id_type=MESH)
+    for dx in range(1, nx):
+        pl.semaphore_signal(
+            barrier, inc=1, device_id={"tgt": lax.rem(x + dx, nx) * CORES + c},
+            device_id_type=MESH)
+    pl.semaphore_signal(
+        barrier, inc=1, device_id={"tgt": x * CORES + 1 - c}, device_id_type=MESH)
+
     def loads(k):
         ks = pl.ds(k * kc, kc)
         return [
@@ -108,13 +119,6 @@
             copy.start()
     for copy in target_loads:
         copy.start()
-
-    barrier = pltpu.get_barrier_semaphore()
-
-    def greet(k):
-        pl.semaphore_signal(barrier, inc=1, device_id=peer(lax.rem(me + k, n)), device_id_type=MESH)
-
-    each(1, n, greet)
 
     strata = strata_ref[...].astype(F32)
     live = jnp.logical_and(keep_ref[...] == 1, iota((1, examples), 1) < cnt_ref[0])
@@ -143,13 +147,10 @@
         lax.rem(iota((rows, kr), 0), kr) == iota((rows, kr), 1)
     ).astype(BF16)
 
-    pl.semaphore_wait(barrier, n - 1)
-
     def count_copy(k):
         return pltpu.make_async_remote_copy(
             crow, cbuf.at[me], ns, nr, device_id=peer(lax.rem(me + k, n)), device_id_type=MESH)
 
-    each(1, n, lambda k: count_copy(k).start())
     cbuf[me] = own_counts
 
     span = sel.shape[0]
@@ -201,7 +202,9 @@
         down_f = dot(mix_down, wh.astype(BF16)).astype(BF16)
         sbuf[half, :, :, 0:hw] = up_f.reshape(nz, CAP * kr, hw)
         sbuf[half, :, :, hw:2 * hw] = down_f.reshape(nz, CAP * kr, hw)
-        for k in range(nz - 1, 0, -1):
+        if half == 0:
+            pl.semaphore_wait(barrier, nz + nx - 1)
+        for k in range(1, nz):
             z_copy(half, k).start()
         spread_out(half, sbuf.at[half, z], z)
         xbuf[half, c, x, z] = sbuf[half, z]
@@ -223,15 +226,17 @@
 
     for copy in target_loads:
         copy.wait()
-    total = None
-    for r in range(kr):
-        v = tup[r].astype(F32)
-        total = v * v if total is None else total + v * v
-    for q in range(up_len // kd):
-        v = tdr[:, q * kd:(q + 1) * kd].astype(F32)
-        total = total + v * v
-    target_scale = math.sqrt(2.0 * up_len) * lax.rsqrt(
-        jnp.sum(total, axis=1, keepdims=True) + EPSILON)
+
+    def target_scales():
+        total = None
+        for r in range(kr):
+            v = tup[r].astype(F32)
+            total = v * v if total is None else total + v * v
+        for q in range(up_len // kd):
+            v = tdr[:, q * kd:(q + 1) * kd].astype(F32)
+            total = total + v * v
+        return math.sqrt(2.0 * up_len) * lax.rsqrt(
+            jnp.sum(total, axis=1, keepdims=True) + EPSILON)
 
     def arrange(q):
         piece = dot(tdr[:, q * span:(q + 1) * span], sel[...]).astype(BF16)
@@ -254,6 +259,7 @@
             device_id={"tgt": origin_x * CORES + c}, device_id_type=MESH).wait_recv()
         c_copy(half, block, origin_x, origin_z).start()
 
+    target_scale = target_scales()
     pieces = up_len // span
     todo = [lambda q=q: arrange(q) for q in range(pieces)]
     steps = []
@@ -279,6 +285,8 @@
     for half in range(HALVES):
         other = xbuf.at[half, 1 - c]
         pltpu.make_async_copy(other, other, cr.at[half]).wait()
+        if half == 0:
+            each(1, n, lambda k: count_copy(k).start())
         block = xbuf[half].reshape(count, 2 * hw)
         cols = slice(half * hw, (half + 1) * hw)
         left = tup[:, :, cols].reshape(kr * local_targets, hw)

time: 27.4 us -> 24.8 us (0.905)
  Pallas kernels: 25.4 us -> 22.8 us
    pallas_call x1, Pallas kernels: 25.4 us -> 22.8 us  [shards(): pl.pallas_call(body, name='select', out_shape=jax.ShapeDtypeStruct((1, ex...]
where the time goes in v3:
time: 24.8 us; the launch traced here: 24.7 us
  Pallas kernels  22.8 us (92%)
  local copies, waits for them, and re-layouts  1.19 us (5%)
  between operations  0.66 us (3%)
    pallas_call x1, Pallas kernels, shards(): pl.pallas_call(body, name='select', out_shape=jax.ShapeDtypeStruct((1, ex...  22.8 us
    unnamed x1, local copies, waits for them, and re-layouts  1.19 us

profile of v3, /device:TPU:0, one launch (start us, length us, event | category | flops | bytes accessed | tf_op | source)
XLA Modules:
  0.0 24.7 jit_solution(14198425232556636744)
XLA Ops:
  0.7 22.8 %select.1 = f32[1,24]{1,0:T(1,128)} custom-call(bf16[192,4096]{1,0:T(8,128)(2,1)} %refs_0_.1, bf16[192,4096]{1,0:T(8,128)(2,1)} %refs_1_.1, bf16[64,4096]{1,0:T(8,128)(2,1)} %bitcast.6, bf16[64,4096]{1,0:T(8,128)(2,1)} %refs_3_.1, bf16[4096,512]{1,0:T(8,128)(2,1)} %refs_4_.1, bf16[8,64]{1,0:T(8,128)(2,1)} %bitcast.7, bf16[1,192,8192]{2,1,0:T(8,128)(2,1)} %refs_6_.1, ...), custom_call_target="tpu_custom_call" | custom-call | tf_op jit(solution)/shard_map/select/pallas_call | solution.py:385
  23.5 1.2 %copy.14 = f32[24]{0:T(128)} copy(f32[24]{0:T(128)} %bitcast.11) | data formatting | bytes 192
